TPU v7x, 128 devices: a whole 4x4x4 slice. The times are simulated.
128 devices in a mesh: gy: 8 (over z_lo, y), gz: 16 (over z_hi, x, core).
Axes of the slice: x: 4, y: 4, z: 4 (z_hi: 2, z_lo: 2; z = z_hi * 2 + z_lo), core: 2. Of those that a mesh axis runs over, the one named last changes fastest.
Arguments:
- fixed_volume: bfloat16 [512, 1024, 1024], P(('gy', 'gz')), may hold values from -16 to 16
- moving_volume: bfloat16 [512, 1024, 1024], P(('gy', 'gz')), may hold values from -16 to 16
- displacement: int32 [3, 32, 32], P(None, 'gz', 'gy'), may hold values from -3 to 3
Outputs:
- residual: float32 [256, 512, 512], P('gz', 'gy')
- gradients: float32 [3, 256, 512, 512], P(None, 'gz', 'gy')
Inputs may be any that keep to these rules, and one draw needn't show every extreme that they name: Each component of a block's displacement lies within -3 to 3, in coarse voxels; blocks are 8 planes by 16 rows by all 512 columns.
All inputs are finite; a program needn't handle non-finite values.
Results may differ from a plain program's by a relative error of at most 0.005.
Values may be sent and summed in bfloat16 or wider, within the bound.
A program may use at most 128 MiB of HBM per device.

v0:
```python
import jax
import jax.numpy as jnp
from jax import lax
from jax.experimental import pallas as pl
from jax.experimental.pallas import tpu as pltpu
from jax.sharding import PartitionSpec as P

MESH = pl.DeviceIdType.MESH
BZ = 8
BY = 16
RIM = 4
LAG = 2
GROUP = 8


def decimate_band(fine_count, coarse_count, first):
    rows = lax.broadcasted_iota(jnp.int32, (fine_count, coarse_count), 0)
    columns = lax.broadcasted_iota(jnp.int32, (fine_count, coarse_count), 1)
    offset = rows - 2 * columns + 2 - first
    weight = jnp.where(
        offset == 2,
        6.0,
        jnp.where(
            (offset == 1) | (offset == 3), 4.0, jnp.where((offset == 0) | (offset == 4), 1.0, 0.0)
        ),
    )
    return (weight / 16.0).astype(jnp.bfloat16)


def gray(m):
    return m + m // 2 - 2 * (m // 3)


def pyramid_kernel(
    fixed, moving, bricks, rims,
    fine, band, partial_x, own, up, down, below, above, coarse, relay,
    in_sem, up_send, up_recv, down_send, down_recv,
    first_send, first_recv, second_send, second_recv, rim_send, rim_recv,
):
    gy = lax.axis_index("gy")
    gz = lax.axis_index("gz")
    zlo, y = gy // 4, gy % 4
    zhi, x, lane = gz // 8, (gz // 2) % 4, gz % 8
    place = gy * 16 + gz
    after = (place + 1) % 128
    before = (place + 127) % 128
    rows_fixed = 64
    rows_moving = rows_fixed + 2 * RIM

    loads = []
    for i in range(8):
        for v, volume in enumerate((fixed, moving)):
            copy = pltpu.make_async_copy(
                volume.at[:, pl.ds(128 * i, 128), :],
                fine.at[v, :, pl.ds(16 + 128 * i, 128), :],
                in_sem.at[v, i],
            )
            copy.start()
            loads.append(copy)

    barrier = pltpu.get_barrier_semaphore()

    def greet(to_gy, to_gz):
        pl.semaphore_signal(barrier, inc=1, device_id=(to_gy, to_gz), device_id_type=MESH)

    for k in range(8):
        greet(k, zlo * 8 + lane)
        greet((gz // 8) * 4 + k // 2, (k % 2) * 8 + lane)
        greet(gy, zhi * 8 + k)
    greet(after // 16, after % 16)
    greet(before // 16, before % 16)

    band[0] = decimate_band(640, 256, 0)
    band[1] = decimate_band(640, 256, 128)
    zero_rows = jnp.zeros((2, 4, 16, 1024), jnp.bfloat16)
    fine[:, :, pl.ds(0, 16), :] = zero_rows
    fine[:, :, pl.ds(1040, 16), :] = zero_rows

    @pl.when(place == 0)
    def _():
        below[...] = jnp.zeros_like(below)

    @pl.when(place == 127)
    def _():
        above[...] = jnp.zeros_like(above)

    def up_copy(k):
        return pltpu.make_async_remote_copy(
            up.at[k], below.at[k], up_send.at[k], up_recv.at[k],
            device_id=(after // 16, after % 16), device_id_type=MESH,
        )

    def down_copy(k):
        return pltpu.make_async_remote_copy(
            down.at[k], above.at[k], down_send.at[k], down_recv.at[k],
            device_id=(before // 16, before % 16), device_id_type=MESH,
        )

    def combine(k):
        @pl.when(place > 0)
        def _():
            up_copy(k).wait_recv()

        @pl.when(place < 127)
        def _():
            down_copy(k).wait_recv()

        coarse[k, 0] = (own[k, 0] + below[k].astype(jnp.float32)).astype(jnp.bfloat16)
        coarse[k, 1] = (own[k, 1] + above[k].astype(jnp.float32) * (1.0 / 16.0)).astype(jnp.bfloat16)

    def wait_band(i):
        for v, volume in enumerate((fixed, moving)):
            pltpu.make_async_copy(
                volume.at[:, pl.ds(0, 128), :], fine.at[v, :, pl.ds(16, 128), :], in_sem.at[v, i]
            ).wait()

    wait_band(0)

    def chunk(k, carry):
        @pl.when(k < 7)
        def _():
            wait_band(k + 1)

        for v in range(2):
            taken = fine[v, :, pl.ds(pl.multiple_of(128 * k, 128), 160), :].reshape(640, 1024)
            for half in range(2):
                product = jnp.dot(
                    taken[:, 384 * half:384 * half + 640], band[half],
                    preferred_element_type=jnp.float32,
                )
                product = product.astype(jnp.bfloat16).astype(jnp.float32)
                for q in range(2):
                    partial_x[v, :, 2 * half + q] = product[:, 128 * q:128 * q + 128].reshape(4, 160, 128)
        for v in range(2):
            count = rows_moving if v else rows_fixed
            base = 8 if v else 16
            put = rows_fixed if v else 0
            for q in range(4):
                cols = pl.ds(128 * q, 128)
                half_planes = []
                for p in range(4):
                    tap = [
                        partial_x[v, p, q, pl.ds(base + t - 2, count, stride=2), :] for t in range(5)
                    ]
                    total = (
                        (tap[0] + tap[4]) * 0.0625 + (tap[1] + tap[3]) * 0.25 + tap[2] * 0.375
                    )
                    half_planes.append(total.astype(jnp.bfloat16))
                down[k, pl.ds(put, count), cols] = half_planes[0]
                a0, a1, a2, a3 = [h.astype(jnp.float32) for h in half_planes]
                tail = a2 * 0.0625 + a3 * 0.25
                up[k, pl.ds(put, count), cols] = tail.astype(jnp.bfloat16)
                own[k, 0, pl.ds(put, count), cols] = a0 * 0.375 + a1 * 0.25 + a2 * 0.0625
                own[k, 1, pl.ds(put, count), cols] = (
                    a0 * 0.0625 + a1 * 0.25 + a2 * 0.375 + a3 * 0.25
                )

        @pl.when(k == 0)
        def _():
            pl.semaphore_wait(barrier, 26)

        @pl.when(place < 127)
        def _():
            up_copy(k).start()

        @pl.when(place > 0)
        def _():
            down_copy(k).start()

        @pl.when(k >= LAG)
        def _():
            combine(k - LAG)

        return carry

    lax.fori_loop(0, 8, chunk, 0)
    for k in range(8 - LAG, 8):
        combine(k)

    slot = y * 2 + zhi

    def first_target(i):
        row = (y + gray(i // 2) + 4 - x) % 4
        j = ((i % 2 + zlo) % 2) * 4 + row
        return j, (j == gy) & (zlo == zhi)

    def first_copy(i):
        j, _ = first_target(i)
        return pltpu.make_async_remote_copy(
            coarse.at[j], relay.at[slot], first_send.at[i], first_recv.at[slot],
            device_id=(j, zlo * 8 + lane), device_id_type=MESH,
        )

    def send_first(i, carry):
        j, stays = first_target(i)

        @pl.when(stays)
        def _():
            pltpu.make_async_copy(coarse.at[j], relay.at[slot], first_recv.at[slot]).start()

        @pl.when(jnp.logical_not(stays))
        def _():
            first_copy(i).start()

        return carry

    lax.fori_loop(0, 8, send_first, 0)

    def second_target(i):
        source = (y + 4 - gray(i // 2) + x) % 4
        return source * 2 + i % 2

    def second_copy(i):
        t = second_target(i)
        return pltpu.make_async_remote_copy(
            relay.at[t], bricks.at[lane], second_send.at[i], second_recv.at[lane],
            device_id=(gy, zhi * 8 + t), device_id_type=MESH,
        )

    def send_second(i, carry):
        t = second_target(i)
        pltpu.make_async_copy(coarse.at[0], relay.at[t], first_recv.at[t]).wait()

        @pl.when(t == lane)
        def _():
            pltpu.make_async_copy(relay.at[t], bricks.at[lane], second_recv.at[lane]).start()

        @pl.when(t != lane)
        def _():
            second_copy(i).start()

        return carry

    lax.fori_loop(0, 8, send_second, 0)

    def rim_copy(side, i, s):
        target = gz - 1 if side else gz + 1
        return pltpu.make_async_remote_copy(
            bricks.at[s, :, pl.ds(rows_fixed, rows_moving), :], rims.at[side, i],
            rim_send.at[side, i], rim_recv.at[side, i],
            device_id=(gy, target), device_id_type=MESH,
        )

    def finish(i, carry):
        source = (x + 4 - y + gray(i // 2)) % 4
        s = source * 2 + i % 2
        pltpu.make_async_copy(relay.at[0], bricks.at[s], second_recv.at[s]).wait()

        @pl.when((source == 3) & (gz < 15))
        def _():
            rim_copy(0, i % 2, s).start()

        @pl.when((source == 0) & (gz > 0))
        def _():
            rim_copy(1, i % 2, s).start()

        return carry

    lax.fori_loop(0, 8, finish, 0)

    def drain(k, carry):
        @pl.when(place < 127)
        def _():
            up_copy(k).wait_send()

        @pl.when(place > 0)
        def _():
            down_copy(k).wait_send()

        @pl.when(jnp.logical_not(first_target(k)[1]))
        def _():
            first_copy(k).wait_send()

        @pl.when(second_target(k) != lane)
        def _():
            second_copy(k).wait_send()

        return carry

    lax.fori_loop(0, 8, drain, 0)
    for i in range(2):
        @pl.when(gz < 15)
        def _():
            rim_copy(0, i, 6 + i).wait_send()
            rim_copy(1, i, i).wait_recv()

        @pl.when(gz > 0)
        def _():
            rim_copy(1, i, i).wait_send()
            rim_copy(0, i, 6 + i).wait_recv()


def exchange(fixed_volume, moving_volume):
    bf16 = jnp.bfloat16
    rows = 136
    dma = pltpu.SemaphoreType.DMA
    return pl.pallas_call(
        pyramid_kernel,
        out_shape=[
            jax.ShapeDtypeStruct((8, 2, rows, 512), bf16),
            jax.ShapeDtypeStruct((2, 2, 2, 72, 512), bf16),
        ],
        in_specs=[pl.BlockSpec(memory_space=pl.ANY)] * 2,
        out_specs=[pl.BlockSpec(memory_space=pl.ANY)] * 2,
        scratch_shapes=[
            pltpu.VMEM((2, 4, 1056, 1024), bf16),
            pltpu.VMEM((2, 640, 256), bf16),
            pltpu.VMEM((2, 4, 4, 160, 128), jnp.float32),
            pltpu.VMEM((8, 2, rows, 512), jnp.float32),
            pltpu.VMEM((8, rows, 512), bf16),
            pltpu.VMEM((8, rows, 512), bf16),
            pltpu.VMEM((8, rows, 512), bf16),
            pltpu.VMEM((8, rows, 512), bf16),
            pltpu.VMEM((8, 2, rows, 512), bf16),
            pltpu.VMEM((8, 2, rows, 512), bf16),
            dma((2, 8)),
            dma((8,)), dma((8,)), dma((8,)), dma((8,)),
            dma((8,)), dma((8,)), dma((8,)), dma((8,)),
            dma((2, 2)), dma((2, 2)),
        ],
        compiler_params=pltpu.CompilerParams(
            collective_id=0, has_side_effects=True, vmem_limit_bytes=60 * 2**20
        ),
        name="pyramid",
    )(fixed_volume, moving_volume)


def warp_kernel(moves, bricks, rims, residual, gradients, grid):
    gy = lax.axis_index("gy")
    gz = lax.axis_index("gz")
    block = pl.program_id(0)
    rows = 72

    def put(at, plane):
        for q in range(4):
            grid[at, q] = plane[:, 128 * q:128 * q + 128]

    @pl.when(block == 0)
    def _():
        row = lax.broadcasted_iota(jnp.int32, (rows, 512), 0)
        inside = ((row >= RIM) | (gy > 0)) & ((row < rows - RIM) | (gy < 7))
        for s in range(8):
            for p in range(2):
                plane = bricks[s, p, 64:136, :].astype(jnp.float32)
                put(RIM + 2 * s + p, jnp.where(inside, plane, 0.0))
        for side in range(2):
            there = inside & (gz < 15 if side else gz > 0)
            for i in range(2):
                for p in range(2):
                    plane = rims[side, i, p].astype(jnp.float32)
                    put(side * 20 + 2 * i + p, jnp.where(there, plane, 0.0))

    bz = block // 4
    by = block % 4
    dz = moves[0, bz, by]
    dy = moves[1, bz, by]
    dx = moves[2, bz, by]
    plane0 = bz * BZ + RIM + dz
    row0 = by * BY + RIM + dy
    column = lax.broadcasted_iota(jnp.int32, (BY, 512), 1)

    def shifted(values, by_columns):
        rolled = pltpu.roll(values, (512 - by_columns) % 512, 1)
        at = column + by_columns
        return jnp.where((at >= 0) & (at < 512), rolled, 0.0)

    def window(plane, row):
        return jnp.concatenate([grid[plane, q, pl.ds(row, BY), :] for q in range(4)], axis=1)

    center = [shifted(window(plane0 + i - 1, row0), dx) for i in range(BZ + 2)]
    for i in range(BZ):
        fixed = bricks[4 * bz + i // 2, i % 2, pl.ds(pl.multiple_of(by * BY, BY), BY), :]
        residual[i] = center[i + 1] - fixed.astype(jnp.float32)
        gradients[0, i] = (center[i + 2] - center[i]) * 0.5
        following = window(plane0 + i, row0 + 1)
        preceding = window(plane0 + i, row0 - 1)
        gradients[1, i] = shifted((following - preceding) * 0.5, dx)
        here = window(plane0 + i, row0)
        gradients[2, i] = (shifted(here, dx + 1) - shifted(here, dx - 1)) * 0.5


def warp(displacement, bricks, rims):
    f32 = jnp.float32
    return pl.pallas_call(
        warp_kernel,
        grid=(8,),
        out_shape=[
            jax.ShapeDtypeStruct((16, 64, 512), f32),
            jax.ShapeDtypeStruct((3, 16, 64, 512), f32),
        ],
        in_specs=[
            pl.BlockSpec(memory_space=pltpu.SMEM),
            pl.BlockSpec(memory_space=pltpu.VMEM),
            pl.BlockSpec(memory_space=pltpu.VMEM),
        ],
        out_specs=[
            pl.BlockSpec((BZ, BY, 512), lambda b: (b // 4, b % 4, 0)),
            pl.BlockSpec((3, BZ, BY, 512), lambda b: (0, b // 4, b % 4, 0)),
        ],
        scratch_shapes=[pltpu.VMEM((24, 4, 72, 128), f32)],
        name="warp",
    )(displacement, bricks, rims)


def shards(fixed_volume, moving_volume, displacement):
    bricks, rims = exchange(fixed_volume, moving_volume)
    residual, gradients = warp(displacement, bricks, rims)
    return residual, gradients


def solution(mesh):
    placed = (P(("gy", "gz"), None, None), P(("gy", "gz"), None, None), P(None, "gz", "gy"))
    return jax.shard_map(
        shards,
        mesh=mesh,
        in_specs=placed,
        out_specs=(P("gz", "gy", None), P(None, "gz", "gy", None)),
        check_vma=False,
    )
```

profile of v0, /device:TPU:73, one launch (start us, length us, event | category | flops | bytes accessed | tf_op | source)
XLA Modules:
  0.0 104.5 jit_solution(18380648587533758961)
XLA Ops:
  0.6 95.8 %pyramid.1 = (bf16[8,2,136,512]{3,2,1,0:T(8,128)(2,1)}, bf16[2,2,2,72,512]{4,3,2,1,0:T(8,128)(2,1)}) custom-call(bf16[4,1024,1024]{2,1,0:T(8,128)(2,1)} %fixed.1, bf16[4,1024,1024]{2,1,0:T(8,128)(2,1)} %moving.1), custom_call_target="tpu_custom_call" | custom-call | tf_op jit(solution)/shard_map/pyramid/pallas_call | solution.py:297
  96.4 8.0 %warp.1 = (f32[16,64,512]{2,1,0:T(8,128)}, f32[3,16,64,512]{3,2,1,0:T(8,128)}) custom-call(s32[3,2,4]{2,1,0:T(2,128)} %moves.1, bf16[8,2,136,512]{3,2,1,0:T(8,128)(2,1)} %get-tuple-element.4.bricks, bf16[2,2,2,72,512]{4,3,2,1,0:T(8,128)(2,1)} %get-tuple-element.5.rims), custom_call_target="tpu_custom_call" | custom-call | tf_op jit(solution)/shard_map/warp/pallas_call | solution.py:384
where the time goes:
time: 105 us; the launch traced here: 104 us
  Pallas kernels  104 us (99%)
    pallas_call x1, Pallas kernels, exchange(): pl.pallas_call(pyramid_kernel, out_shape=[jax.ShapeDtypeStruct((8, 2, row...  95.8 us
    pallas_call x1, Pallas kernels, warp(): pl.pallas_call(warp_kernel, grid=(8,), out_shape=[jax.ShapeDtypeStruct((1...  8.01 us

commit v1 on v0

--- a/solution.py
+++ b/solution.py
@@ -10,7 +10,7 @@
 BY = 16
 RIM = 4
 LAG = 2
-GROUP = 8
+RELAY_LAG = 4
 
 
 def decimate_band(fine_count, coarse_count, first):
@@ -33,9 +33,9 @@
 
 def pyramid_kernel(
     fixed, moving, bricks, rims,
-    fine, band, partial_x, own, up, down, below, above, coarse, relay,
+    fine, band, partial_x, own, up, down, below, above, coarse, column, relay,
     in_sem, up_send, up_recv, down_send, down_recv,
-    first_send, first_recv, second_send, second_recv, rim_send, rim_recv,
+    row_send, row_recv, depth_send, depth_recv, second_send, second_recv, rim_send, rim_recv,
 ):
     gy = lax.axis_index("gy")
     gz = lax.axis_index("gz")
@@ -64,9 +64,12 @@
         pl.semaphore_signal(barrier, inc=1, device_id=(to_gy, to_gz), device_id_type=MESH)
 
     for k in range(8):
-        greet(k, zlo * 8 + lane)
-        greet((gz // 8) * 4 + k // 2, (k % 2) * 8 + lane)
         greet(gy, zhi * 8 + k)
+    for k in range(4):
+        greet(zlo * 4 + k, gz)
+    for k in range(2):
+        greet(k * 4 + y, zlo * 8 + lane)
+        greet(zhi * 4 + y, k * 8 + lane)
     greet(after // 16, after % 16)
     greet(before // 16, before % 16)
 
@@ -157,7 +160,7 @@
 
         @pl.when(k == 0)
         def _():
-            pl.semaphore_wait(barrier, 26)
+            pl.semaphore_wait(barrier, 18)
 
         @pl.when(place < 127)
         def _():
@@ -177,34 +180,61 @@
     for k in range(8 - LAG, 8):
         combine(k)
 
-    slot = y * 2 + zhi
-
-    def first_target(i):
-        row = (y + gray(i // 2) + 4 - x) % 4
-        j = ((i % 2 + zlo) % 2) * 4 + row
-        return j, (j == gy) & (zlo == zhi)
-
-    def first_copy(i):
-        j, _ = first_target(i)
-        return pltpu.make_async_remote_copy(
-            coarse.at[j], relay.at[slot], first_send.at[i], first_recv.at[slot],
-            device_id=(j, zlo * 8 + lane), device_id_type=MESH,
-        )
-
-    def send_first(i, carry):
-        j, stays = first_target(i)
+    def row_target(i):
+        return (y + gray(i // 2) + 4 - x) % 4, (i % 2 + zlo) % 2
+
+    def row_copy(i):
+        row, part = row_target(i)
+        return pltpu.make_async_remote_copy(
+            coarse.at[part * 4 + row], column.at[y * 2 + part],
+            row_send.at[i], row_recv.at[y * 2 + part],
+            device_id=(zlo * 4 + row, gz), device_id_type=MESH,
+        )
+
+    def send_row(i, carry):
+        row, part = row_target(i)
+
+        @pl.when(row == y)
+        def _():
+            pltpu.make_async_copy(
+                coarse.at[part * 4 + row], column.at[y * 2 + part], row_recv.at[y * 2 + part]
+            ).start()
+
+        @pl.when(row != y)
+        def _():
+            row_copy(i).start()
+
+        return carry
+
+    lax.fori_loop(0, 8, send_row, 0)
+
+    def depth_target(i):
+        source = (y + 4 - gray(i // 2) + x) % 4
+        part = (i % 2 + zlo) % 2
+        return source, part, (part == zlo) & (zlo == zhi)
+
+    def depth_copy(i):
+        source, part, _ = depth_target(i)
+        return pltpu.make_async_remote_copy(
+            column.at[source * 2 + part], relay.at[source * 2 + zhi],
+            depth_send.at[i], depth_recv.at[source * 2 + zhi],
+            device_id=(part * 4 + y, zlo * 8 + lane), device_id_type=MESH,
+        )
+
+    def send_depth(i):
+        source, part, stays = depth_target(i)
+        slot = source * 2 + part
+        pltpu.make_async_copy(coarse.at[0], column.at[slot], row_recv.at[slot]).wait()
 
         @pl.when(stays)
         def _():
-            pltpu.make_async_copy(coarse.at[j], relay.at[slot], first_recv.at[slot]).start()
+            pltpu.make_async_copy(
+                column.at[slot], relay.at[source * 2 + zhi], depth_recv.at[source * 2 + zhi]
+            ).start()
 
         @pl.when(jnp.logical_not(stays))
         def _():
-            first_copy(i).start()
-
-        return carry
-
-    lax.fori_loop(0, 8, send_first, 0)
+            depth_copy(i).start()
 
     def second_target(i):
         source = (y + 4 - gray(i // 2) + x) % 4
@@ -217,9 +247,9 @@
             device_id=(gy, zhi * 8 + t), device_id_type=MESH,
         )
 
-    def send_second(i, carry):
+    def send_second(i):
         t = second_target(i)
-        pltpu.make_async_copy(coarse.at[0], relay.at[t], first_recv.at[t]).wait()
+        pltpu.make_async_copy(column.at[0], relay.at[t], depth_recv.at[t]).wait()
 
         @pl.when(t == lane)
         def _():
@@ -229,9 +259,18 @@
         def _():
             second_copy(i).start()
 
+    def pass_on(i, carry):
+        @pl.when(i < 8)
+        def _():
+            send_depth(i)
+
+        @pl.when(i >= RELAY_LAG)
+        def _():
+            send_second(i - RELAY_LAG)
+
         return carry
 
-    lax.fori_loop(0, 8, send_second, 0)
+    lax.fori_loop(0, 8 + RELAY_LAG, pass_on, 0)
 
     def rim_copy(side, i, s):
         target = gz - 1 if side else gz + 1
@@ -267,9 +306,13 @@
         def _():
             down_copy(k).wait_send()
 
-        @pl.when(jnp.logical_not(first_target(k)[1]))
-        def _():
-            first_copy(k).wait_send()
+        @pl.when(row_target(k)[0] != y)
+        def _():
+            row_copy(k).wait_send()
+
+        @pl.when(jnp.logical_not(depth_target(k)[2]))
+        def _():
+            depth_copy(k).wait_send()
 
         @pl.when(second_target(k) != lane)
         def _():
@@ -313,9 +356,10 @@
             pltpu.VMEM((8, rows, 512), bf16),
             pltpu.VMEM((8, 2, rows, 512), bf16),
             pltpu.VMEM((8, 2, rows, 512), bf16),
+            pltpu.VMEM((8, 2, rows, 512), bf16),
             dma((2, 8)),
             dma((8,)), dma((8,)), dma((8,)), dma((8,)),
-            dma((8,)), dma((8,)), dma((8,)), dma((8,)),
+            dma((8,)), dma((8,)), dma((8,)), dma((8,)), dma((8,)), dma((8,)),
             dma((2, 2)), dma((2, 2)),
         ],
         compiler_params=pltpu.CompilerParams(

time: 105 us -> 99.5 us (0.948)
  the two profiles are of different devices: /device:TPU:73 before, /device:TPU:33 now
where the time goes in v1:
time: 99.5 us; the launch traced here: 99.4 us
  Pallas kernels  98.8 us (99%)
    pallas_call x1, Pallas kernels, exchange(): pl.pallas_call(pyramid_kernel, out_shape=[jax.ShapeDtypeStruct((8, 2, row...  90.8 us
    pallas_call x1, Pallas kernels, warp(): pl.pallas_call(warp_kernel, grid=(8,), out_shape=[jax.ShapeDtypeStruct((1...  8.01 us

profile of v1, /device:TPU:33, one launch (start us, length us, event | category | flops | bytes accessed | tf_op | source)
XLA Modules:
  0.0 99.4 jit_solution(11647263655588918005)
XLA Ops:
  0.6 90.8 %pyramid.1 = (bf16[8,2,136,512]{3,2,1,0:T(8,128)(2,1)}, bf16[2,2,2,72,512]{4,3,2,1,0:T(8,128)(2,1)}) custom-call(bf16[4,1024,1024]{2,1,0:T(8,128)(2,1)} %fixed.1, bf16[4,1024,1024]{2,1,0:T(8,128)(2,1)} %moving.1), custom_call_target="tpu_custom_call" | custom-call | tf_op jit(solution)/shard_map/pyramid/pallas_call | solution.py:340
  91.4 8.0 %warp.1 = (f32[16,64,512]{2,1,0:T(8,128)}, f32[3,16,64,512]{3,2,1,0:T(8,128)}) custom-call(s32[3,2,4]{2,1,0:T(2,128)} %moves.1, bf16[8,2,136,512]{3,2,1,0:T(8,128)(2,1)} %get-tuple-element.4.bricks, bf16[2,2,2,72,512]{4,3,2,1,0:T(8,128)(2,1)} %get-tuple-element.5.rims), custom_call_target="tpu_custom_call" | custom-call | tf_op jit(solution)/shard_map/warp/pallas_call | solution.py:428

commit v2 on v1

--- a/solution.py
+++ b/solution.py
@@ -181,7 +181,7 @@
         combine(k)
 
     def row_target(i):
-        return (y + gray(i // 2) + 4 - x) % 4, (i % 2 + zlo) % 2
+        return (y + gray(i // 2)) % 4, (i % 2 + zlo) % 2
 
     def row_copy(i):
         row, part = row_target(i)
@@ -209,7 +209,7 @@
     lax.fori_loop(0, 8, send_row, 0)
 
     def depth_target(i):
-        source = (y + 4 - gray(i // 2) + x) % 4
+        source = (y + 4 - gray(i // 2)) % 4
         part = (i % 2 + zlo) % 2
         return source, part, (part == zlo) & (zlo == zhi)
 
@@ -237,7 +237,7 @@
             depth_copy(i).start()
 
     def second_target(i):
-        source = (y + 4 - gray(i // 2) + x) % 4
+        source = (y + 4 - gray(i // 2)) % 4
         return source * 2 + i % 2
 
     def second_copy(i):

time: 99.5 us -> 94.3 us (0.948)
  the two profiles are of different devices: /device:TPU:33 before, /device:TPU:92 now
where the time goes in v2:
time: 94.3 us; the launch traced here: 94.2 us
  Pallas kernels  93.6 us (99%)
    pallas_call x1, Pallas kernels, exchange(): pl.pallas_call(pyramid_kernel, out_shape=[jax.ShapeDtypeStruct((8, 2, row...  85.6 us
    pallas_call x1, Pallas kernels, warp(): pl.pallas_call(warp_kernel, grid=(8,), out_shape=[jax.ShapeDtypeStruct((1...  8.01 us

profile of v2, /device:TPU:92, one launch (start us, length us, event | category | flops | bytes accessed | tf_op | source)
XLA Modules:
  0.0 94.2 jit_solution(17397479330000187922)
XLA Ops:
  0.6 85.6 %pyramid.1 = (bf16[8,2,136,512]{3,2,1,0:T(8,128)(2,1)}, bf16[2,2,2,72,512]{4,3,2,1,0:T(8,128)(2,1)}) custom-call(bf16[4,1024,1024]{2,1,0:T(8,128)(2,1)} %fixed.1, bf16[4,1024,1024]{2,1,0:T(8,128)(2,1)} %moving.1), custom_call_target="tpu_custom_call" | custom-call | tf_op jit(solution)/shard_map/pyramid/pallas_call | solution.py:340
  86.2 8.0 %warp.1 = (f32[16,64,512]{2,1,0:T(8,128)}, f32[3,16,64,512]{3,2,1,0:T(8,128)}) custom-call(s32[3,2,4]{2,1,0:T(2,128)} %moves.1, bf16[8,2,136,512]{3,2,1,0:T(8,128)(2,1)} %get-tuple-element.4.bricks, bf16[2,2,2,72,512]{4,3,2,1,0:T(8,128)(2,1)} %get-tuple-element.5.rims), custom_call_target="tpu_custom_call" | custom-call | tf_op jit(solution)/shard_map/warp/pallas_call | solution.py:428
